TPU v7x, 128 devices: a whole 4x4x4 slice. The times are simulated.
128 devices in a mesh: space: 32 (over z, y_hi, x), sample: 4 (over y_lo, core).
Axes of the slice: x: 4, y: 4 (y_hi: 2, y_lo: 2; y = y_hi * 2 + y_lo), z: 4, core: 2. Of those that a mesh axis runs over, the one named last changes fastest.
Arguments:
- state_hat: float32 [20, 3, 256, 32, 128], P('sample', None, 'space'), may hold values from -2.4 to 2.4
- adjoint_hat: float32 [20, 3, 256, 32, 128], P('sample', None, 'space'), may hold values from -2.4 to 2.4
- objective_hat: float32 [20, 3, 256, 32, 128], P('sample', None, 'space'), may hold values from -6 to 6
- density: float32 [256, 32, 128], P('space'), may hold values from 0.05 to 1
- region: int32 [256, 32, 128], P('space'), may hold values from 0 to 3
Outputs:
- adjoint_residual: float32 [20, 3, 256, 32, 128], P('sample', None, 'space')
- density_gradient: float32 [256, 32, 128], P('space', 'sample')
All inputs are finite; a program needn't handle non-finite values.
Results may differ from a plain program's by a relative error of at most 0.00026.
Values sent between devices are 32-bit elements; how exact they have to be, the bound alone decides.
A program may use at most 128 MiB of HBM per device.

v0:
```python
import math
import jax
import jax.numpy as jnp
from jax import lax
from jax.sharding import PartitionSpec as P

NCOEF = 20
NT = 40
magnet_reluct = 0.95
iron_floor = 0.05
saturation = 1.0


def passed_along(array, axis, by):
    size = lax.axis_size(axis)
    pairs = [(i, i + by) for i in range(size) if 0 <= i + by < size]
    return lax.ppermute(array, axis, pairs)


def harmonic_table():
    sample_steps = jnp.arange(NT, dtype=jnp.int32).astype(jnp.float32)
    orders = (jnp.arange(NCOEF // 2, dtype=jnp.int32) + 1).astype(jnp.float32)
    angles = 2.0 * math.pi / NT * sample_steps[:, None] * orders[None, :]
    return jnp.stack([jnp.cos(angles), jnp.sin(angles)], axis=2).reshape(NT, NCOEF)


def forward_diff(potential, along):
    length = potential.shape[along]
    widths = [(0, 0)] * potential.ndim
    widths[along] = (0, 1)
    padded = jnp.pad(potential, widths)
    return lax.slice_in_dim(padded, 1, length + 1, axis=along) - potential


def backward_diff(potential, along):
    length = potential.shape[along]
    widths = [(0, 0)] * potential.ndim
    widths[along] = (1, 0)
    padded = jnp.pad(potential, widths)
    return lax.slice_in_dim(padded, 0, length, axis=along) - potential


def curl_field(potential, upper):
    x_step = jnp.concatenate([potential[:, :, 1:], upper], axis=2) - potential
    part_one, part_two, part_three = (potential[:, 0], potential[:, 1], potential[:, 2])
    flux_one = forward_diff(part_three, 2) - forward_diff(part_two, 3)
    flux_two = forward_diff(part_one, 3) - x_step[:, 2]
    flux_three = x_step[:, 1] - forward_diff(part_one, 2)
    return jnp.stack([flux_one, flux_two, flux_three], axis=1)


def curl_back(field_h, lower):
    x_step = jnp.concatenate([lower, field_h[:, 1:3, :-1]], axis=2) - field_h[:, 1:3]
    back_one = backward_diff(field_h[:, 1], 3) - backward_diff(field_h[:, 2], 2)
    back_two = x_step[:, 1] - backward_diff(field_h[:, 0], 3)
    back_three = backward_diff(field_h[:, 0], 2) - x_step[:, 0]
    return jnp.stack([back_one, back_two, back_three], axis=1)


def material(density, region):
    iron_share = jnp.where(region == 0, density**3, jnp.zeros_like(density))
    iron_slope = jnp.where(region == 0, 3.0 * density**2, jnp.zeros_like(density))
    base_reluct = jnp.where(
        region == 1, magnet_reluct * jnp.ones_like(density), jnp.ones_like(density)
    )
    return (iron_share, iron_slope, base_reluct)


def reluctivity(state_flux, adjoint_flux, base_reluct, iron_share):
    flux_square = jnp.sum(state_flux * state_flux, axis=1)
    flux_inner = jnp.sum(state_flux * adjoint_flux, axis=1)
    iron_curve = iron_floor + (1.0 - iron_floor) * flux_square / (flux_square + saturation)
    curve_slope = (1.0 - iron_floor) * saturation / (flux_square + saturation) ** 2
    reluct_now = base_reluct + iron_share * (iron_curve - 1.0)
    reluct_slope = iron_share * curve_slope
    field_h = (
        reluct_now[:, None] * adjoint_flux + (2.0 * reluct_slope * flux_inner)[:, None] * state_flux
    )
    return (field_h, iron_curve, flux_inner)


def local(state_hat, adjoint_hat, objective_hat, density, region):
    harm_table = harmonic_table()
    groups = lax.axis_size("sample")
    local_times = NT // groups
    planes = state_hat.shape[2]
    first_time = lax.axis_index("sample") * local_times
    own_rows = lax.dynamic_slice_in_dim(harm_table, first_time, local_times, 0)
    iron_share, iron_slope, base_reluct = material(density, region)
    columns = own_rows
    state_time = jnp.tensordot(
        columns,
        lax.all_gather(state_hat, "sample", axis=0, tiled=True),
        axes=1,
        precision=lax.Precision.HIGHEST,
    )
    adjoint_time = jnp.tensordot(
        columns,
        lax.all_gather(adjoint_hat, "sample", axis=0, tiled=True),
        axes=1,
        precision=lax.Precision.HIGHEST,
    )
    first_planes = jnp.concatenate([state_time[:, :, :1], adjoint_time[:, :, :1]], axis=1)
    upper = passed_along(first_planes, "space", -1)
    state_flux = curl_field(state_time, upper[:, :3])
    adjoint_flux = curl_field(adjoint_time, upper[:, 3:])
    field_h, iron_curve, flux_inner = reluctivity(state_flux, adjoint_flux, base_reluct, iron_share)
    lower = passed_along(field_h[:, 1:3, planes - 1 :], "space", 1)
    back_field = curl_back(field_h, lower)
    partial_terms = -(1.0 / NT) * jnp.sum(iron_slope * (iron_curve - 1.0) * flux_inner, axis=0)
    columns = own_rows
    summed = lax.psum_scatter(
        2.0 / NT * jnp.tensordot(columns.T, back_field, axes=1, precision=lax.Precision.HIGHEST),
        "sample",
        scatter_dimension=0,
        tiled=True,
    )
    density_gradient = lax.psum_scatter(partial_terms, "sample", scatter_dimension=1, tiled=True)
    adjoint_residual = objective_hat - summed
    return (adjoint_residual, density_gradient)


def solution(mesh):
    in_specs = (
        P("sample", None, "space", None, None),
        P("sample", None, "space", None, None),
        P("sample", None, "space", None, None),
        P("space", None, None),
        P("space", None, None),
    )
    out_specs = (P("sample", None, "space", None, None), P("space", "sample", None))
    return jax.shard_map(local, mesh=mesh, in_specs=in_specs, out_specs=out_specs, check_vma=False)
```

profile of v0, /device:TPU:1, one launch (start us, length us, event | category | flops | bytes accessed | tf_op | source)
XLA Modules:
  0.0 376.0 jit_solution(5956820325559077423)
XLA Ops:
  7.2 0.7 all-gather.3.cloned.1.call-update
  8.0 0.7 all-gather.5.cloned.1.call-update
  9.0 0.8 fusion.43
  9.8 80.5 %all-gather.3.cloned.1.call-done = f32[20,3,8,32,128]{4,3,2,1,0:T(8,128)} async-done(((f32[5,3,8,32,128]{4,3,2,1,0:T(8,128)}), f32[20,3,8,32,128]{4,3,2,1,0:T(8,128)}) %all-gather.3.cloned.1.call-update) | async-done | bytes 7864336 | tf_op jit(solution)/shard_map/all_gather | solution.py:93
  90.3 14.4 %fusion.2 = f32[10,3,8,32,128]{4,0,3,2,1:T(8,128)S(1)} fusion(f32[20,3,8,32,128]{4,3,2,1,0:T(8,128)} %all-gather.3.cloned.1.call-done, f32[40,20]{0,1:T(8,128)S(1)} %reshape.127, s32[]{:T(128)S(6)} %select_n.13), kind=kOutput, calls=%fused_computation.2 | convolution fusion | flops 235929600 | bytes 11799684 | tf_op jit(solution)/shard_map/dot_general | solution.py:91
  104.8 2.8 copy-done
  107.6 62.3 %all-gather.5.cloned.1.call-done = f32[20,3,8,32,128]{4,3,2,1,0:T(8,128)} async-done(((f32[5,3,8,32,128]{4,3,2,1,0:T(8,128)}), f32[20,3,8,32,128]{4,3,2,1,0:T(8,128)}) %all-gather.5.cloned.1.call-update) | async-done | bytes 7864336 | tf_op jit(solution)/shard_map/all_gather | solution.py:99
  169.9 14.4 %fusion = f32[10,3,8,32,128]{4,0,3,2,1:T(8,128)S(1)} fusion(f32[20,3,8,32,128]{4,3,2,1,0:T(8,128)} %all-gather.5.cloned.1.call-done, f32[40,20]{0,1:T(8,128)S(1)} %reshape.127, s32[]{:T(128)S(6)} %select_n.13), kind=kOutput, calls=%fused_computation | convolution fusion | flops 235929600 | bytes 11799684 | tf_op jit(solution)/shard_map/dot_general | solution.py:97
  184.9 1.3 collective-permute-start
  186.2 0.9 fusion.42
  187.0 2.2 slice-done
  189.2 0.7 slice-done.1
  189.9 2.8 slice_bitcast_fusion.13
  192.7 3.4 slice_bitcast_fusion.8
  196.1 13.5 %collective-permute-done = f32[10,6,1,32,128]{4,3,2,1,0:T(8,128)S(1)} collective-permute-done((f32[10,6,1,32,128]{4,3,2,1,0:T(8,128)S(1)}, f32[10,6,1,32,128]{4,3,2,1,0:T(8,128)S(1)}, u32[]{:S(2)}, u32[]{:S(2)}) %collective-permute-start) | collective-permute-done | bytes 983072 | tf_op jit(solution)/shard_map/ppermute | solution.py:17
  210.0 1.2 copy.26
  211.2 3.8 %maximum_subtract_fusion = f32[10,3,8,32,128]{4,0,3,2,1:T(8,128)} fusion(f32[10,3,8,32,128]{4,0,3,2,1:T(8,128)S(1)} %bitcast.77, f32[10,3,1,32,128]{4,0,3,2,1:T(8,128)S(1)} %copy.25, f32[10,3,7,32,128]{4,0,3,2,1:T(8,128)S(1)} %slice-done.4), kind=kLoop, calls=%fused_computation.4 | loop fusion | flops 1966080 | bytes 11796480 | tf_op jit(solution)/shard_map/sub | solution.py:44
  215.4 6.8 %maximum_subtract_fusion.1 = f32[10,3,8,32,128]{4,0,3,2,1:T(8,128)} fusion(f32[10,3,8,32,128]{4,0,3,2,1:T(8,128)} %copy-done.1, f32[10,3,1,32,128]{4,0,3,2,1:T(8,128)} %copy.26, f32[10,3,7,32,128]{4,0,3,2,1:T(8,128)S(1)} %slice-done.5), kind=kLoop, calls=%fused_computation.6 | loop fusion | flops 1966080 | bytes 11796480 | tf_op jit(solution)/shard_map/sub | solution.py:44
  222.3 5.8 %fusion.33 = (f32[10,1,8,32,128]{4,0,3,2,1:T(8,128)S(1)}, f32[10,1,8,32,128]{4,0,3,2,1:T(8,128)S(1)}, f32[10,1,8,32,128]{4,0,3,2,1:T(8,128)S(1)}) fusion(f32[10,8,32,128]{3,0,2,1:T(8,128)} %get-tuple-element.20, f32[10,3,8,32,128]{4,0,3,2,1:T(8,128)S(1)} %copy-done.2, f32[10,8,32,128]{3,0,2,1:T(8,128)S(1)} %copy-done.6, f32[10,8,32,128]{3,0,2,1:T(8,128)} %get-tuple-element.21), kind=kLoop, calls=%fused_computation.52 | loop fusion | flops 2293760 | bytes 10485760 | tf_op jit(solution)/shard_map/stack | solution.py:49
  230.0 1.7 fusion.37
  231.7 2.0 multiply_reduce_fusion.1
  233.8 1.6 multiply_reduce_fusion.2
  235.4 1.1 multiply_add_fusion
  237.4 3.1 collective-permute-start.1
  241.2 10.5 %collective-permute-done.1 = f32[10,2,1,32,128]{4,0,3,2,1:T(8,128)S(1)} collective-permute-done((f32[10,2,1,32,128]{4,0,3,2,1:T(8,128)S(1)}, f32[10,2,1,32,128]{4,0,3,2,1:T(8,128)S(1)}, u32[]{:S(2)}, u32[]{:S(2)}) %collective-permute-start.1) | collective-permute-done | bytes 327712 | tf_op jit(solution)/shard_map/ppermute | solution.py:17
  252.3 0.7 fusion.41
  253.1 8.6 %broadcast_multiply_fusion = f32[20,3,8,32,128]{4,0,3,2,1:T(8,128)S(1)} fusion(f32[10,1,8,32,128]{4,0,3,2,1:T(8,128)S(1)} %get-tuple-element.18, f32[10,1,8,32,128]{4,0,3,2,1:T(8,128)S(1)} %get-tuple-element.17, f32[10,1,8,32,128]{4,0,3,2,1:T(8,128)S(1)} %fusion.26, f32[40,20]{0,1:T(8,128)S(1)} %reshape.127, s32[]{:T(128)S(6)} %select_n.13), kind=kOutput, calls=%fused_computation.17 | convolution fusion | flops 239861760 | bytes 11799684 | tf_op jit(solution)/shard_map/dot_general | solution.py:113
  261.7 4.5 %copy.22 = f32[20,3,8,32,128]{4,3,2,1,0:T(8,128)} copy(f32[20,3,8,32,128]{4,0,3,2,1:T(8,128)S(1)} %broadcast_multiply_fusion) | data formatting | bytes 15728640 | tf_op jit(solution)/shard_map/mul | solution.py:113
  266.3 0.7 broadcast_multiply_fusion.1
  267.0 81.5 %reduce-scatter.3.cloned.1.call-done = f32[5,3,8,32,128]{4,3,2,1,0:T(8,128)} async-done(((f32[20,3,8,32,128]{4,3,2,1,0:T(8,128)}), f32[5,3,8,32,128]{4,3,2,1,0:T(8,128)}) %reduce-scatter.3.cloned.1.call-update) | async-done | bytes 1966096 | tf_op jit(solution)/shard_map/reduce_scatter | solution.py:112
  348.4 3.3 sub.107
  351.7 17.7 %reduce-scatter.5.cloned.1.call-done = f32[8,8,128]{2,1,0:T(8,128)} async-done(((f32[8,32,128]{2,1,0:T(8,128)}), f32[8,8,128]{2,1,0:T(8,128)}) %reduce-scatter.5.cloned.1.call-update) | async-done | bytes 32784 | tf_op jit(solution)/shard_map/reduce_scatter | solution.py:118
  (64 shorter events, 5.7 us)
Async XLA Ops:
  7.2 1.8 copy-start.11
  7.2 1.8 copy-start.12
  7.2 83.1 %all-gather.3.cloned.1.call-start = ((), (), s32[]{:S(2)}) async-start(), calls=%async_computation.2 | async-start | bytes 9830400 | tf_op jit(solution)/shard_map/all_gather | solution.py:93
  7.9 162.0 %all-gather.5.cloned.1.call-start = ((), (), s32[]{:S(2)}) async-start(), calls=%async_computation.3 | async-start | bytes 9830400 | tf_op jit(solution)/shard_map/all_gather | solution.py:99
  8.7 339.8 %reduce-scatter.3.cloned.1.call-start = ((), (), s32[]{:S(2)}) async-start(), calls=%async_computation.4 | async-start | bytes 9830400 | tf_op jit(solution)/shard_map/reduce_scatter | solution.py:112
  104.8 2.8 copy-start
  184.3 8.4 %copy-start.1 = (f32[10,3,8,32,128]{4,0,3,2,1:T(8,128)}, f32[10,3,8,32,128]{4,0,3,2,1:T(8,128)S(1)}, u32[]{:S(2)}) copy-start(f32[10,3,8,32,128]{4,0,3,2,1:T(8,128)S(1)} %fusion) | copy-start | bytes 11796484
  184.9 24.8 %collective-permute-start = (f32[10,6,1,32,128]{4,3,2,1,0:T(8,128)S(1)}, f32[10,6,1,32,128]{4,3,2,1,0:T(8,128)S(1)}, u32[]{:S(2)}, u32[]{:S(2)}) collective-permute-start(f32[10,6,1,32,128]{4,3,2,1,0:T(8,128)S(1)} %copy.19), channel_id=1, source_target_pairs={{4,0},{8,4},{12,8},{16,12},{20,16},{24,20},{28,24},{32,28},{36,32}... | collective-permute-start | bytes 2949128 | tf_op jit(solution)/shard_map/ppermute | solution.py:17
  187.0 2.2 slice-start
  187.0 2.9 slice-start.1
  189.9 21.3 %slice-start.2 = ((s8[6291456]{0:T(1024)(128)(4,1)}), s8[2097152]{0:T(1024)(128)(4,1)S(1)}, s32[]{:S(2)}) async-start(s8[6291456]{0:T(1024)(128)(4,1)} %bitcast.76), calls=%async_computation.8 | async-start | bytes 4194304
  192.7 18.5 %slice-start.3 = ((s8[6291456]{0:T(1024)(128)(4,1)}), s8[4194304]{0:T(1024)(128)(4,1)S(1)}, s32[]{:S(2)}) async-start(s8[6291456]{0:T(1024)(128)(4,1)} %bitcast.76), calls=%async_computation.9 | async-start | bytes 8388608
  192.7 18.5 %slice-start.4 = ((f32[10,3,8,32,128]{4,0,3,2,1:T(8,128)}), f32[10,3,7,32,128]{4,0,3,2,1:T(8,128)S(1)}, s32[]{:S(2)}) async-start(f32[10,3,8,32,128]{4,0,3,2,1:T(8,128)} %copy-done), calls=%async_computation.10 | async-start | bytes 11010048 | tf_op jit(solution)/shard_map/slice | solution.py:44
  211.2 4.2 %slice-start.5 = ((f32[10,3,8,32,128]{4,0,3,2,1:T(8,128)}), f32[10,3,7,32,128]{4,0,3,2,1:T(8,128)S(1)}, s32[]{:S(2)}) async-start(f32[10,3,8,32,128]{4,0,3,2,1:T(8,128)} %copy-done.1), calls=%async_computation.11 | async-start | bytes 11010048 | tf_op jit(solution)/shard_map/slice | solution.py:44
  215.4 6.8 %copy-start.2 = (f32[10,3,8,32,128]{4,0,3,2,1:T(8,128)S(1)}, f32[10,3,8,32,128]{4,0,3,2,1:T(8,128)}, u32[]{:S(2)}) copy-start(f32[10,3,8,32,128]{4,0,3,2,1:T(8,128)} %maximum_subtract_fusion) | copy-start | bytes 11796484
  215.4 6.8 %copy-start.6 = (f32[10,8,32,128]{3,0,2,1:T(8,128)S(1)}, f32[10,8,32,128]{3,0,2,1:T(8,128)}, u32[]{:S(2)}) copy-start(f32[10,8,32,128]{3,0,2,1:T(8,128)} %get-tuple-element.19) | copy-start | bytes 3932164
  222.3 5.9 %slice-start.6 = ((s8[6291456]{0:T(1024)(128)(4,1)}), s8[4194304]{0:T(1024)(128)(4,1)S(1)}, s32[]{:S(2)}) async-start(s8[6291456]{0:T(1024)(128)(4,1)} %bitcast.78), calls=%async_computation.12 | async-start | bytes 8388608
  222.3 5.9 %slice-start.7 = ((s8[6291456]{0:T(1024)(128)(4,1)}), s8[2097152]{0:T(1024)(128)(4,1)S(1)}, s32[]{:S(2)}) async-start(s8[6291456]{0:T(1024)(128)(4,1)} %bitcast.78), calls=%async_computation.13 | async-start | bytes 4194304
  222.3 6.5 %copy-start.3 = (f32[10,8,32,128]{3,0,2,1:T(8,128)S(1)}, f32[10,8,32,128]{3,0,2,1:T(8,128)}, u32[]{:S(2)}) copy-start(f32[10,8,32,128]{3,0,2,1:T(8,128)} %get-tuple-element.22) | copy-start | bytes 3932164
  222.3 7.1 %copy-start.4 = (f32[10,8,32,128]{3,0,2,1:T(8,128)S(1)}, f32[10,8,32,128]{3,0,2,1:T(8,128)}, u32[]{:S(2)}) copy-start(f32[10,8,32,128]{3,0,2,1:T(8,128)} %get-tuple-element.23) | copy-start | bytes 3932164
  222.3 7.7 %copy-start.5 = (f32[10,8,32,128]{3,0,2,1:T(8,128)S(1)}, f32[10,8,32,128]{3,0,2,1:T(8,128)}, u32[]{:S(2)}) copy-start(f32[10,8,32,128]{3,0,2,1:T(8,128)} %get-tuple-element.24) | copy-start | bytes 3932164
  231.7 2.1 copy-start.8
  231.7 2.1 copy-start.9
  231.7 2.1 copy-start.10
  237.4 14.3 %collective-permute-start.1 = (f32[10,2,1,32,128]{4,0,3,2,1:T(8,128)S(1)}, f32[10,2,1,32,128]{4,0,3,2,1:T(8,128)S(1)}, u32[]{:S(2)}, u32[]{:S(2)}) collective-permute-start(f32[10,2,1,32,128]{4,0,3,2,1:T(8,128)S(1)} %slice.163), channel_id=1, source_target_pairs={{0,4},{4,8},{8,12},{12,16},{16,20},{20,24},{24,28},{28,32},{32,36}... | collective-permute-start | bytes 983048 | tf_op jit(solution)/shard_map/ppermute | solution.py:17
  266.2 82.2 %copy-start.7 = (f32[5,3,8,32,128]{4,3,2,1,0:T(8,128)S(1)}, f32[5,3,8,32,128]{4,3,2,1,0:T(8,128)}, u32[]{:S(2)}) copy-start(f32[5,3,8,32,128]{4,3,2,1,0:T(8,128)} %param.7) | copy-start | bytes 5898244
  266.2 103.2 %reduce-scatter.5.cloned.1.call-start = ((), (), s32[]{:S(2)}) async-start(), calls=%async_computation.5 | async-start | bytes 163840 | tf_op jit(solution)/shard_map/reduce_scatter | solution.py:118
Sparse Core Ops, SparseCore 0:
  9.7 80.6 all-gather.2
  92.0 77.8 all-gather.4
  266.4 82.0 reduce-scatter.2
  351.2 18.1 reduce-scatter.4
where the time goes:
time: 376 us
  waiting for transfers between devices  268 us (71%)
  matrix products  37.5 us (10%)
  other arithmetic  30.8 us (8%)
  local copies, waits for them, and re-layouts  21.4 us (6%)
  between operations  14.1 us (4%)
  starting transfers between devices  4.57 us (1%)
    reduce_scatter x1, waiting for transfers between devices, local(): lax.psum_scatter(2.0 / NT * jnp.tensordot(columns.T, back_field, axes=1,...  81.5 us
    all_gather x1, waiting for transfers between devices, local(): lax.all_gather(state_hat, 'sample', axis=0, tiled=True)  80.5 us
    all_gather x1, waiting for transfers between devices, local(): lax.all_gather(adjoint_hat, 'sample', axis=0, tiled=True)  62.3 us
    ppermute x2, waiting for transfers between devices, passed_along(): return lax.ppermute(array, axis, pairs)  24.1 us
    reduce_scatter x1, waiting for transfers between devices, local(): lax.psum_scatter(partial_terms, 'sample', scatter_dimension=1, tiled=True)  17.7 us
    dot_general x1, matrix products, local(): jnp.tensordot(columns, lax.all_gather(state_hat, 'sample', axis=0, tiled=...  14.4 us
    dot_general x1, matrix products, local(): jnp.tensordot(columns, lax.all_gather(adjoint_hat, 'sample', axis=0, tile...  14.4 us
    sub x2, other arithmetic, curl_field(): x_step = jnp.concatenate([potential[:, :, 1:], upper], axis=2) - potential  10.7 us
  transfers between devices with their start and end apart: 6, of which 6 were waited for; matrix products, arithmetic and copies ran while one was open for 7% of the time, Pallas kernels for 0%

commit v1 on v0

--- a/solution.py
+++ b/solution.py
@@ -1,3 +1,4 @@
+import functools
 import math
 import jax
 import jax.numpy as jnp
@@ -9,6 +10,21 @@
 magnet_reluct = 0.95
 iron_floor = 0.05
 saturation = 1.0
+
+
+def pairs_all_connect(array_here, device_axis, d0):
+    return jnp.concatenate(
+        lax.all_to_all(
+            jnp.stack(lax.axis_size(device_axis) * [array_here], axis=0),
+            axis_name=device_axis,
+            split_axis=0,
+            concat_axis=0,
+        ),
+        axis=d0,
+    )
+
+
+_define_steps_all = functools.partial(pairs_all_connect, device_axis="sample", d0=0)
 
 
 def passed_along(array, axis, by):
@@ -89,10 +105,7 @@
     iron_share, iron_slope, base_reluct = material(density, region)
     columns = own_rows
     state_time = jnp.tensordot(
-        columns,
-        lax.all_gather(state_hat, "sample", axis=0, tiled=True),
-        axes=1,
-        precision=lax.Precision.HIGHEST,
+        columns, _define_steps_all(state_hat), axes=1, precision=lax.Precision.HIGHEST
     )
     adjoint_time = jnp.tensordot(
         columns,

time: 376 us -> 411 us (1.093); the launches traced: 376 us -> 405 us
  other arithmetic: 30.8 us -> 43 us
  starting transfers between devices: 4.57 us -> 11.9 us
  waiting for transfers between devices: 268 us -> 274 us
    all_to_all x0 -> x1, waiting for transfers between devices: none -> 149 us  [pairs_all_connect(): lax.all_to_all(jnp.stack(lax.axis_size(device_axis) * [array_here], axis=...]
    all_gather x1 -> x0, waiting for transfers between devices: 80.5 us -> none  [local(): lax.all_gather(state_hat, 'sample', axis=0, tiled=True)]
    all_gather x1, waiting for transfers between devices: 62.3 us -> 0.02 us  [local(): lax.all_gather(adjoint_hat, 'sample', axis=0, tiled=True)]
    another operation x2, other arithmetic: 7.55 us -> 19.9 us  [curl_field(): return jnp.stack([flux_one, flux_two, flux_three], axis=1)]
    all_to_all x0 -> x1, starting transfers between devices: none -> 7.05 us  [pairs_all_connect(): lax.all_to_all(jnp.stack(lax.axis_size(device_axis) * [array_here], axis=...]
    another operation x0 -> x1, local copies, waits for them, and re-layouts: none -> 4.16 us  [pairs_all_connect(): jnp.stack(lax.axis_size(device_axis) * [array_here], axis=0)]
    unnamed x40 -> x42, local copies, waits for them, and re-layouts: 8.95 us -> 7.51 us
  transfers between devices with their start and end apart: 6 -> 6, of which waited for: 6 -> 5; matrix products, arithmetic and copies ran while one was open for 7% -> 8% of each run, Pallas kernels for 0% -> 0%
where the time goes in v1:
time: 411 us; the launch traced here: 405 us
  waiting for transfers between devices  274 us (67%)
  other arithmetic  43 us (10%)
  matrix products  37.8 us (9%)
  local copies, waits for them, and re-layouts  24.1 us (6%)
  between operations  14.1 us (3%)
  starting transfers between devices  11.9 us (3%)
    all_to_all x1, waiting for transfers between devices, pairs_all_connect(): lax.all_to_all(jnp.stack(lax.axis_size(device_axis) * [array_here], axis=...  149 us
    reduce_scatter x1, waiting for transfers between devices, local(): lax.psum_scatter(2.0 / NT * jnp.tensordot(columns.T, back_field, axes=1,...  84.3 us
    ppermute x2, waiting for transfers between devices, passed_along(): return lax.ppermute(array, axis, pairs)  22.5 us
    another operation x2, other arithmetic, curl_field(): return jnp.stack([flux_one, flux_two, flux_three], axis=1)  19.9 us
    reduce_scatter x1, waiting for transfers between devices, local(): lax.psum_scatter(partial_terms, 'sample', scatter_dimension=1, tiled=True)  17.9 us
    dot_general x1, matrix products, local(): jnp.tensordot(columns, lax.all_gather(adjoint_hat, 'sample', axis=0, tile...  14.8 us
    dot_general x1, matrix products, local(): jnp.tensordot(columns, _define_steps_all(state_hat), axes=1, precision=la...  14.4 us
    sub x2, other arithmetic, curl_field(): x_step = jnp.concatenate([potential[:, :, 1:], upper], axis=2) - potential  10.7 us
  transfers between devices with their start and end apart: 6, of which 5 were waited for; matrix products, arithmetic and copies ran while one was open for 8% of the time, Pallas kernels for 0%

profile of v1, /device:TPU:1, one launch (start us, length us, event | category | flops | bytes accessed | tf_op | source)
XLA Modules:
  0.0 405.3 jit_solution(3140519439670424233)
XLA Ops:
  7.2 0.7 all-gather.2.cloned.1.call-update
  7.9 0.8 copy-done.7
  8.7 4.2 %stack.49 = f32[4,5,3,8,32,128]{5,4,3,2,1,0:T(8,128)} broadcast(f32[5,3,8,32,128]{4,3,2,1,0:T(8,128)S(1)} %copy-done.7), dimensions={1,2,3,4,5} | broadcast | bytes 9830400 | tf_op jit(solution)/shard_map/stack | solution.py:18
  12.9 7.1 %all-to-all-start = ((f32[4,5,3,8,32,128]{5,4,3,2,1,0:T(8,128)}), f32[4,5,3,8,32,128]{5,4,3,2,1,0:T(8,128)}, u32[]{:S(2)}, u32[]{:S(2)}) async-start(f32[4,5,3,8,32,128]{5,4,3,2,1,0:T(8,128)} %stack.49), calls=%async_computation | async-start | bytes 15728640 | tf_op jit(solution)/shard_map/all_to_all | solution.py:17
  20.2 0.8 fusion.43
  21.0 148.7 %all-to-all-done = f32[4,5,3,8,32,128]{5,4,3,2,1,0:T(8,128)} async-done(((f32[4,5,3,8,32,128]{5,4,3,2,1,0:T(8,128)}), f32[4,5,3,8,32,128]{5,4,3,2,1,0:T(8,128)}, u32[]{:S(2)}, u32[]{:S(2)}) %all-to-all-start) | async-done | bytes 7864352 | tf_op jit(solution)/shard_map/all_to_all | solution.py:17
  169.7 14.4 %fusion.2 = f32[10,3,8,32,128]{4,0,3,2,1:T(8,128)S(1)} fusion(f32[20,3,8,32,128]{4,3,2,1,0:T(8,128)} %bitcast.3, f32[40,20]{0,1:T(8,128)S(1)} %reshape.132, s32[]{:T(128)S(6)} %select_n.13), kind=kOutput, calls=%fused_computation.2 | convolution fusion | flops 235929600 | bytes 11799684 | tf_op jit(solution)/shard_map/dot_general | solution.py:107
  184.2 2.7 copy-done
  186.9 14.8 %fusion = f32[10,3,8,32,128]{4,0,3,2,1:T(8,128)S(1)} fusion(f32[20,3,8,32,128]{4,3,2,1,0:T(8,128)} %all-gather.2.cloned.1.call-done, f32[40,20]{0,1:T(8,128)S(1)} %reshape.132, s32[]{:T(128)S(6)} %select_n.13), kind=kOutput, calls=%fused_computation | convolution fusion | flops 235929600 | bytes 11799684 | tf_op jit(solution)/shard_map/dot_general | solution.py:110
  202.3 1.6 collective-permute-start
  203.8 0.7 fusion.42
  204.5 1.7 slice-done
  206.2 0.8 slice-done.1
  207.0 2.8 slice_bitcast_fusion.13
  209.8 3.4 slice_bitcast_fusion.8
  213.2 13.7 %collective-permute-done = f32[10,6,1,32,128]{4,3,2,1,0:T(8,128)S(1)} collective-permute-done((f32[10,6,1,32,128]{4,3,2,1,0:T(8,128)S(1)}, f32[10,6,1,32,128]{4,3,2,1,0:T(8,128)S(1)}, u32[]{:S(2)}, u32[]{:S(2)}) %collective-permute-start) | collective-permute-done | bytes 983072 | tf_op jit(solution)/shard_map/ppermute | solution.py:33
  227.3 1.2 copy.26
  228.5 3.8 maximum_subtract_fusion
  232.7 6.8 %maximum_subtract_fusion.1 = f32[10,3,8,32,128]{4,0,3,2,1:T(8,128)} fusion(f32[10,3,8,32,128]{4,0,3,2,1:T(8,128)} %copy-done.1, f32[10,3,1,32,128]{4,0,3,2,1:T(8,128)} %copy.26, f32[10,3,7,32,128]{4,0,3,2,1:T(8,128)S(1)} %slice-done.5), kind=kLoop, calls=%fused_computation.6 | loop fusion | flops 1966080 | bytes 11796480 | tf_op jit(solution)/shard_map/sub | solution.py:60
  239.6 18.2 %fusion.33 = (f32[10,1,8,32,128]{4,0,3,2,1:T(8,128)S(1)}, f32[10,1,8,32,128]{4,0,3,2,1:T(8,128)S(1)}, f32[10,1,8,32,128]{4,0,3,2,1:T(8,128)S(1)}) fusion(f32[10,8,32,128]{3,0,2,1:T(8,128)} %get-tuple-element.20, f32[10,3,8,32,128]{4,0,3,2,1:T(8,128)S(1)} %copy-done.2, f32[10,8,32,128]{3,0,2,1:T(8,128)S(1)} %copy-done.6, f32[10,8,32,128]{3,0,2,1:T(8,128)} %get-tuple-element.21), kind=kLoop, calls=%fused_computation.52 | loop fusion | flops 2293760 | bytes 10485760 | tf_op jit(solution)/shard_map/stack | solution.py:65
  257.9 1.7 fusion.37
  259.6 2.0 multiply_reduce_fusion.1
  261.7 1.6 multiply_reduce_fusion.2
  263.3 1.1 multiply_add_fusion
  265.3 3.3 collective-permute-start.1
  269.2 8.8 %collective-permute-done.1 = f32[10,2,1,32,128]{4,0,3,2,1:T(8,128)S(1)} collective-permute-done((f32[10,2,1,32,128]{4,0,3,2,1:T(8,128)S(1)}, f32[10,2,1,32,128]{4,0,3,2,1:T(8,128)S(1)}, u32[]{:S(2)}, u32[]{:S(2)}) %collective-permute-start.1) | collective-permute-done | bytes 327712 | tf_op jit(solution)/shard_map/ppermute | solution.py:33
  278.6 0.7 fusion.41
  279.4 8.6 %broadcast_multiply_fusion = f32[20,3,8,32,128]{4,0,3,2,1:T(8,128)S(1)} fusion(f32[10,1,8,32,128]{4,0,3,2,1:T(8,128)S(1)} %get-tuple-element.18, f32[10,1,8,32,128]{4,0,3,2,1:T(8,128)S(1)} %get-tuple-element.17, f32[10,1,8,32,128]{4,0,3,2,1:T(8,128)S(1)} %fusion.26, f32[40,20]{0,1:T(8,128)S(1)} %reshape.132, s32[]{:T(128)S(6)} %select_n.13), kind=kOutput, calls=%fused_computation.17 | convolution fusion | flops 239861760 | bytes 11799684 | tf_op jit(solution)/shard_map/dot_general | solution.py:126
  288.0 4.5 %copy.22 = f32[20,3,8,32,128]{4,3,2,1,0:T(8,128)} copy(f32[20,3,8,32,128]{4,0,3,2,1:T(8,128)S(1)} %broadcast_multiply_fusion) | data formatting | bytes 15728640 | tf_op jit(solution)/shard_map/mul | solution.py:126
  293.3 84.3 %reduce-scatter.3.cloned.1.call-done = f32[5,3,8,32,128]{4,3,2,1,0:T(8,128)} async-done(((f32[20,3,8,32,128]{4,3,2,1,0:T(8,128)}), f32[5,3,8,32,128]{4,3,2,1,0:T(8,128)}) %reduce-scatter.3.cloned.1.call-update) | async-done | bytes 1966096 | tf_op jit(solution)/shard_map/reduce_scatter | solution.py:125
  377.6 3.3 sub.107
  380.9 17.9 %reduce-scatter.5.cloned.1.call-done = f32[8,8,128]{2,1,0:T(8,128)} async-done(((f32[8,32,128]{2,1,0:T(8,128)}), f32[8,8,128]{2,1,0:T(8,128)}) %reduce-scatter.5.cloned.1.call-update) | async-done | bytes 32784 | tf_op jit(solution)/shard_map/reduce_scatter | solution.py:131
  (66 shorter events, 4.6 us)
Async XLA Ops:
  7.2 1.5 copy-start.7
  7.2 179.8 %all-gather.2.cloned.1.call-start = ((), (), s32[]{:S(2)}) async-start(), calls=%async_computation.3 | async-start | bytes 9830400 | tf_op jit(solution)/shard_map/all_gather | solution.py:112
  12.9 7.3 %copy-start.12 = (f32[8,32,128]{2,1,0:T(8,128)S(1)}, f32[8,32,128]{2,1,0:T(8,128)}, u32[]{:S(2)}) copy-start(f32[8,32,128]{2,1,0:T(8,128)} %param.8) | copy-start | bytes 393220
  12.9 7.3 %copy-start.13 = (s32[8,32,128]{2,1,0:T(8,128)S(1)}, s32[8,32,128]{2,1,0:T(8,128)}, u32[]{:S(2)}) copy-start(s32[8,32,128]{2,1,0:T(8,128)} %param.9) | copy-start | bytes 393220
  12.9 156.9 %all-to-all-start = ((f32[4,5,3,8,32,128]{5,4,3,2,1,0:T(8,128)}), f32[4,5,3,8,32,128]{5,4,3,2,1,0:T(8,128)}, u32[]{:S(2)}, u32[]{:S(2)}) async-start(f32[4,5,3,8,32,128]{5,4,3,2,1,0:T(8,128)} %stack.49), calls=%async_computation | async-start | bytes 15728640 | tf_op jit(solution)/shard_map/all_to_all | solution.py:17
  19.9 357.7 %reduce-scatter.3.cloned.1.call-start = ((), (), s32[]{:S(2)}) async-start(), calls=%async_computation.4 | async-start | bytes 9830400 | tf_op jit(solution)/shard_map/reduce_scatter | solution.py:125
  184.2 2.7 copy-start
  201.7 8.1 %copy-start.1 = (f32[10,3,8,32,128]{4,0,3,2,1:T(8,128)}, f32[10,3,8,32,128]{4,0,3,2,1:T(8,128)S(1)}, u32[]{:S(2)}) copy-start(f32[10,3,8,32,128]{4,0,3,2,1:T(8,128)S(1)} %fusion) | copy-start | bytes 11796484
  201.9 4.3 %slice-start = ((s8[6291456]{0:T(1024)(128)(4,1)}), s8[4194304]{0:T(1024)(128)(4,1)S(1)}, s32[]{:S(2)}) async-start(s8[6291456]{0:T(1024)(128)(4,1)} %bitcast.75), calls=%async_computation.6 | async-start | bytes 8388608
  202.3 24.6 %collective-permute-start = (f32[10,6,1,32,128]{4,3,2,1,0:T(8,128)S(1)}, f32[10,6,1,32,128]{4,3,2,1,0:T(8,128)S(1)}, u32[]{:S(2)}, u32[]{:S(2)}) collective-permute-start(f32[10,6,1,32,128]{4,3,2,1,0:T(8,128)S(1)} %copy.19), channel_id=1, source_target_pairs={{4,0},{8,4},{12,8},{16,12},{20,16},{24,20},{28,24},{32,28},{36,32}... | collective-permute-start | bytes 2949128 | tf_op jit(solution)/shard_map/ppermute | solution.py:33
  204.5 2.5 slice-start.1
  209.8 18.7 %slice-start.2 = ((s8[6291456]{0:T(1024)(128)(4,1)}), s8[4194304]{0:T(1024)(128)(4,1)S(1)}, s32[]{:S(2)}) async-start(s8[6291456]{0:T(1024)(128)(4,1)} %bitcast.77), calls=%async_computation.8 | async-start | bytes 8388608
  209.8 18.7 %slice-start.3 = ((s8[6291456]{0:T(1024)(128)(4,1)}), s8[2097152]{0:T(1024)(128)(4,1)S(1)}, s32[]{:S(2)}) async-start(s8[6291456]{0:T(1024)(128)(4,1)} %bitcast.77), calls=%async_computation.9 | async-start | bytes 4194304
  209.8 18.7 %slice-start.4 = ((f32[10,3,8,32,128]{4,0,3,2,1:T(8,128)}), f32[10,3,7,32,128]{4,0,3,2,1:T(8,128)S(1)}, s32[]{:S(2)}) async-start(f32[10,3,8,32,128]{4,0,3,2,1:T(8,128)} %copy-done), calls=%async_computation.10 | async-start | bytes 11010048 | tf_op jit(solution)/shard_map/slice | solution.py:60
  228.5 4.2 %slice-start.5 = ((f32[10,3,8,32,128]{4,0,3,2,1:T(8,128)}), f32[10,3,7,32,128]{4,0,3,2,1:T(8,128)S(1)}, s32[]{:S(2)}) async-start(f32[10,3,8,32,128]{4,0,3,2,1:T(8,128)} %copy-done.1), calls=%async_computation.11 | async-start | bytes 11010048 | tf_op jit(solution)/shard_map/slice | solution.py:60
  232.7 6.8 %copy-start.2 = (f32[10,3,8,32,128]{4,0,3,2,1:T(8,128)S(1)}, f32[10,3,8,32,128]{4,0,3,2,1:T(8,128)}, u32[]{:S(2)}) copy-start(f32[10,3,8,32,128]{4,0,3,2,1:T(8,128)} %maximum_subtract_fusion) | copy-start | bytes 11796484
  232.7 6.8 %copy-start.6 = (f32[10,8,32,128]{3,0,2,1:T(8,128)S(1)}, f32[10,8,32,128]{3,0,2,1:T(8,128)}, u32[]{:S(2)}) copy-start(f32[10,8,32,128]{3,0,2,1:T(8,128)} %get-tuple-element.19) | copy-start | bytes 3932164
  239.5 18.3 %slice-start.6 = ((s8[6291456]{0:T(1024)(128)(4,1)}), s8[4194304]{0:T(1024)(128)(4,1)S(1)}, s32[]{:S(2)}) async-start(s8[6291456]{0:T(1024)(128)(4,1)} %bitcast.79), calls=%async_computation.12 | async-start | bytes 8388608
  239.6 18.3 %slice-start.7 = ((s8[6291456]{0:T(1024)(128)(4,1)}), s8[2097152]{0:T(1024)(128)(4,1)S(1)}, s32[]{:S(2)}) async-start(s8[6291456]{0:T(1024)(128)(4,1)} %bitcast.79), calls=%async_computation.13 | async-start | bytes 4194304
  239.6 18.3 %copy-start.3 = (f32[10,8,32,128]{3,0,2,1:T(8,128)S(1)}, f32[10,8,32,128]{3,0,2,1:T(8,128)}, u32[]{:S(2)}) copy-start(f32[10,8,32,128]{3,0,2,1:T(8,128)} %get-tuple-element.22) | copy-start | bytes 3932164
  239.6 18.3 %copy-start.4 = (f32[10,8,32,128]{3,0,2,1:T(8,128)S(1)}, f32[10,8,32,128]{3,0,2,1:T(8,128)}, u32[]{:S(2)}) copy-start(f32[10,8,32,128]{3,0,2,1:T(8,128)} %get-tuple-element.23) | copy-start | bytes 3932164
  239.6 18.3 %copy-start.5 = (f32[10,8,32,128]{3,0,2,1:T(8,128)S(1)}, f32[10,8,32,128]{3,0,2,1:T(8,128)}, u32[]{:S(2)}) copy-start(f32[10,8,32,128]{3,0,2,1:T(8,128)} %get-tuple-element.24) | copy-start | bytes 3932164
  259.6 2.1 copy-start.9
  259.6 2.1 copy-start.10
  259.6 2.1 copy-start.11
  265.3 12.7 %collective-permute-start.1 = (f32[10,2,1,32,128]{4,0,3,2,1:T(8,128)S(1)}, f32[10,2,1,32,128]{4,0,3,2,1:T(8,128)S(1)}, u32[]{:S(2)}, u32[]{:S(2)}) collective-permute-start(f32[10,2,1,32,128]{4,0,3,2,1:T(8,128)S(1)} %slice.163), channel_id=1, source_target_pairs={{0,4},{4,8},{8,12},{12,16},{16,20},{20,24},{24,28},{28,32},{32,36}... | collective-permute-start | bytes 983048 | tf_op jit(solution)/shard_map/ppermute | solution.py:33
  292.5 85.1 %copy-start.8 = (f32[5,3,8,32,128]{4,3,2,1,0:T(8,128)S(1)}, f32[5,3,8,32,128]{4,3,2,1,0:T(8,128)}, u32[]{:S(2)}) copy-start(f32[5,3,8,32,128]{4,3,2,1,0:T(8,128)} %param.7) | copy-start | bytes 5898244
  292.5 106.2 %reduce-scatter.5.cloned.1.call-start = ((), (), s32[]{:S(2)}) async-start(), calls=%async_computation.5 | async-start | bytes 163840 | tf_op jit(solution)/shard_map/reduce_scatter | solution.py:131
Sparse Core Ops, SparseCore 0:
  9.6 145.0 all-gather.1
  292.7 84.9 reduce-scatter.2
  380.6 18.1 reduce-scatter.4
